TPU v7x, 32 devices: a whole 2x2x4 slice. The times are simulated.
32 devices in a mesh: dp: 8 (over y, x, core), tensor: 4 (over z).
Axes of the slice: x: 2, y: 2, z: 4, core: 2. Of those that a mesh axis runs over, the one named last changes fastest.
Arguments:
- char_inputs: bfloat16 [131072, 256], P(('dp', 'tensor')), may hold values from -6 to 6
- char_counts: int32 [8192], P(('dp', 'tensor')), may hold values from 1 to 16
- doc_ids: int32 [8, 1024], P('dp'), may hold values from 0 to 3, never falling along the last dimension, each value on 1 to 512 neighbouring positions
- cotangent: bfloat16 [8192, 512], P('dp'), may hold values from -6 to 6
- char_norm_one: float32 [256], replicated, may hold values from 0.5 to 1.5
- char_query: bfloat16 [256, 256], replicated, may hold values from -0.375 to 0.375
- char_key: bfloat16 [256, 256], replicated, may hold values from -0.375 to 0.375
- char_value: bfloat16 [256, 256], replicated, may hold values from -0.375 to 0.375
- char_out: bfloat16 [256, 256], replicated, may hold values from -0.75 to 0.75
- char_norm_two: float32 [256], replicated, may hold values from 0.5 to 1.5
- char_up: bfloat16 [256, 1024], replicated, may hold values from -0.375 to 0.375
- char_down: bfloat16 [1024, 256], replicated, may hold values from -0.1875 to 0.1875
- char_proj: bfloat16 [256, 512], replicated, may hold values from -1.5 to 1.5
- word_norm_one: float32 [512], replicated, may hold values from 0.5 to 1.5
- word_query: bfloat16 [512, 512], P(None, 'tensor'), may hold values from -0.25 to 0.25
- word_key: bfloat16 [512, 512], P(None, 'tensor'), may hold values from -0.25 to 0.25
- word_value: bfloat16 [512, 512], P(None, 'tensor'), may hold values from -0.25 to 0.25
- word_out_proj: bfloat16 [512, 512], P('tensor'), may hold values from -1 to 1
- word_norm_two: float32 [512], replicated, may hold values from 0.5 to 1.5
- word_up: bfloat16 [512, 2048], P(None, 'tensor'), may hold values from -0.25 to 0.25
- word_down: bfloat16 [2048, 512], P('tensor'), may hold values from -0.125 to 0.125
Outputs:
- word_output: bfloat16 [8192, 512], P(('dp', 'tensor'))
- char_input_gradient: float32 [131072, 256], P(('dp', 'tensor'))
- char_norm_one_gradient: float32 [256], replicated
- char_query_gradient: float32 [256, 256], replicated
- char_key_gradient: float32 [256, 256], replicated
- char_value_gradient: float32 [256, 256], replicated
- char_out_gradient: float32 [256, 256], replicated
- char_norm_two_gradient: float32 [256], replicated
- char_up_gradient: float32 [256, 1024], replicated
- char_down_gradient: float32 [1024, 256], replicated
- char_proj_gradient: float32 [256, 512], replicated
- word_norm_one_gradient: float32 [512], replicated
- word_query_gradient: float32 [512, 512], P(None, 'tensor')
- word_key_gradient: float32 [512, 512], P(None, 'tensor')
- word_value_gradient: float32 [512, 512], P(None, 'tensor')
- word_out_proj_gradient: float32 [512, 512], P('tensor')
- word_norm_two_gradient: float32 [512], replicated
- word_up_gradient: float32 [512, 2048], P(None, 'tensor')
- word_down_gradient: float32 [2048, 512], P('tensor')
Inputs may be any that keep to these rules, and one draw needn't show every extreme that they name: Slots of a word from char_counts on are padding. `doc_ids`: ids never fall along a sequence; each document covers 1 to 512 consecutive words, one exactly that many.
All inputs are finite; a program needn't handle non-finite values.
Results may differ from a plain program's by a relative error of at most 0.018.
Values may be sent and summed in bfloat16 or wider, within the bound.
A program may use at most 192 MiB of HBM per device.

v0:
```python
import jax
import jax.numpy as jnp
from jax import lax
from jax.sharding import PartitionSpec as P

HD = 64
CHEADS = 4
CHD = 64
EPSILON = 1e-05
NEG_LARGE = -1e30


def layer_norm(values, gain_vector):
    centre = values - jnp.mean(values, axis=-1, keepdims=True)
    spread = jnp.mean(centre * centre, axis=-1, keepdims=True)
    return centre * lax.rsqrt(spread + EPSILON) * gain_vector


def gelu_tanh(values):
    return jax.nn.gelu(values, approximate=True)


def matmul(left, right):
    return jnp.dot(left, right, preferred_element_type=jnp.float32)


def contract_rows(left, right):
    return lax.dot_general(
        left, right, (((0,), (0,)), ((), ())), preferred_element_type=jnp.float32
    )


def contract_cols(left, right):
    return lax.dot_general(
        left, right, (((1,), (1,)), ((), ())), preferred_element_type=jnp.float32
    )


def block_mask(seq_docs, first_row, block_rows):
    length = seq_docs.shape[0]
    block_docs = lax.dynamic_slice_in_dim(seq_docs, first_row, block_rows, 0)
    row_ids = first_row + jnp.arange(block_rows)
    key_ids = jnp.arange(length)
    return (block_docs[:, None] == seq_docs[None, :]) & (key_ids[None, :] <= row_ids[:, None])


def attention_forward(queries, key_rows, value_rows, doc_ids, block_rows):
    length = queries.shape[1]
    score_scale = queries.shape[3] ** (-0.5)
    block_count = length // block_rows

    def sequence_pass(members):
        seq_q, seq_k, seq_v, seq_docs = members

        def block_pass(block_index):
            first_row = block_index * block_rows
            block_q = lax.dynamic_slice_in_dim(seq_q, first_row, block_rows, 0)
            allowed = block_mask(seq_docs, first_row, block_rows)
            scores = (
                jnp.einsum("qhd,khd->hqk", block_q, seq_k, preferred_element_type=jnp.float32)
                * score_scale
            )
            scores = jnp.where(allowed[None], scores, NEG_LARGE)
            row_max = jnp.max(scores, axis=-1, keepdims=True)
            exponent = jnp.exp(scores - row_max)
            row_total = jnp.sum(exponent, axis=-1, keepdims=True)
            weights_low = (exponent / row_total).astype(jnp.bfloat16)
            mixed_rows = jnp.einsum(
                "hqk,khd->qhd", weights_low, seq_v, preferred_element_type=jnp.float32
            ).astype(jnp.bfloat16)
            return (mixed_rows, (row_max + jnp.log(row_total))[..., 0])

        mixed_rows, log_totals = lax.map(block_pass, jnp.arange(block_count))
        return (mixed_rows.reshape(seq_q.shape), log_totals)

    return lax.map(sequence_pass, (queries, key_rows, value_rows, doc_ids))


def attention_backward(queries, key_rows, value_rows, doc_ids, log_totals, grad_mixed, block_rows):
    length = queries.shape[1]
    score_scale = queries.shape[3] ** (-0.5)
    block_count = length // block_rows

    def sequence_pass(members):
        seq_q, seq_k, seq_v, seq_docs, seq_logs, seq_grad = members

        def block_pass(carried, block_index):
            key_acc, value_acc = carried
            first_row = block_index * block_rows
            block_q = lax.dynamic_slice_in_dim(seq_q, first_row, block_rows, 0)
            block_grad = lax.dynamic_slice_in_dim(seq_grad, first_row, block_rows, 0)
            allowed = block_mask(seq_docs, first_row, block_rows)
            scores = (
                jnp.einsum("qhd,khd->hqk", block_q, seq_k, preferred_element_type=jnp.float32)
                * score_scale
            )
            scores = jnp.where(allowed[None], scores, NEG_LARGE)
            weights_full = jnp.exp(scores - seq_logs[block_index][..., None])
            weights_low = weights_full.astype(jnp.bfloat16)
            value_acc = value_acc + jnp.einsum(
                "hqk,qhd->khd", weights_low, block_grad, preferred_element_type=jnp.float32
            )
            grad_weights = jnp.einsum(
                "qhd,khd->hqk", block_grad, seq_v, preferred_element_type=jnp.float32
            )
            inner_sum = jnp.sum(weights_full * grad_weights, axis=-1, keepdims=True)
            grad_scores = (weights_full * (grad_weights - inner_sum)).astype(jnp.bfloat16)
            grad_block_q = (
                jnp.einsum("hqk,khd->qhd", grad_scores, seq_k, preferred_element_type=jnp.float32)
                * score_scale
            ).astype(jnp.bfloat16)
            key_acc = (
                key_acc
                + jnp.einsum(
                    "hqk,qhd->khd", grad_scores, block_q, preferred_element_type=jnp.float32
                )
                * score_scale
            )
            return ((key_acc, value_acc), grad_block_q)

        zero_rows = jnp.zeros(seq_k.shape, jnp.float32)
        (key_acc, value_acc), grad_q = lax.scan(
            block_pass, (zero_rows, zero_rows), jnp.arange(block_count)
        )
        return (
            grad_q.reshape(seq_q.shape),
            key_acc.astype(jnp.bfloat16),
            value_acc.astype(jnp.bfloat16),
        )

    return lax.map(sequence_pass, (queries, key_rows, value_rows, doc_ids, log_totals, grad_mixed))


def per_device(
    char_inputs,
    char_counts,
    doc_ids,
    cotangent,
    char_norm_one,
    char_query,
    char_key,
    char_value,
    char_out,
    char_norm_two,
    char_up,
    char_down,
    char_proj,
    word_norm_one,
    word_query,
    word_key,
    word_value,
    word_out_proj,
    word_norm_two,
    word_up,
    word_down,
):
    word_count = char_counts.shape[0]
    slot_count = char_inputs.shape[0] // word_count
    char_width = char_inputs.shape[1]
    shape_four = (word_count, slot_count, CHEADS, CHD)
    char_scale = CHD ** (-0.5)
    tensor_rank = lax.axis_index("tensor")
    base_rows = char_inputs.astype(jnp.float32)
    char_normed, pull_char_one = jax.vjp(layer_norm, base_rows, char_norm_one)
    char_normed = char_normed.astype(jnp.bfloat16)
    char_q = matmul(char_normed, char_query).astype(jnp.bfloat16).reshape(shape_four)
    char_k = matmul(char_normed, char_key).astype(jnp.bfloat16).reshape(shape_four)
    char_v = matmul(char_normed, char_value).astype(jnp.bfloat16).reshape(shape_four)
    char_scores = (
        jnp.einsum("wqhd,wkhd->whqk", char_q, char_k, preferred_element_type=jnp.float32)
        * char_scale
    )
    slot_valid = jnp.arange(slot_count)[None, :] < char_counts[:, None]
    char_scores = jnp.where(slot_valid[:, None, None, :], char_scores, NEG_LARGE)
    char_probs = jax.nn.softmax(char_scores, axis=-1)
    char_probs_low = char_probs.astype(jnp.bfloat16)
    char_mixed = jnp.einsum(
        "whqk,wkhd->wqhd", char_probs_low, char_v, preferred_element_type=jnp.float32
    )
    char_mixed = char_mixed.astype(jnp.bfloat16).reshape(word_count * slot_count, char_width)
    char_first = base_rows + matmul(char_mixed, char_out)
    char_normed_two, pull_char_two = jax.vjp(layer_norm, char_first, char_norm_two)
    char_normed_two = char_normed_two.astype(jnp.bfloat16)
    char_hidden, pull_char_gelu = jax.vjp(gelu_tanh, matmul(char_normed_two, char_up))
    char_hidden = char_hidden.astype(jnp.bfloat16)
    char_second = char_first + matmul(char_hidden, char_down)
    slot_weights = slot_valid.astype(jnp.float32) / char_counts.astype(jnp.float32)[:, None]
    pooled = jnp.sum(
        char_second.reshape(word_count, slot_count, char_width) * slot_weights[:, :, None], axis=1
    )
    pooled = pooled.astype(jnp.bfloat16)
    word_vectors = matmul(pooled, char_proj).astype(jnp.bfloat16)
    input_whole = lax.all_gather(word_vectors, "tensor", axis=0, tiled=True).astype(jnp.float32)
    normed_whole, pull_first = jax.vjp(layer_norm, input_whole, word_norm_one)
    normed = normed_whole.astype(jnp.bfloat16)
    sequences = doc_ids.shape[0]
    seq_len = doc_ids.shape[1]
    token_count = sequences * seq_len
    head_count = word_query.shape[1] // HD
    shape_heads = (sequences, seq_len, head_count, HD)
    block_rows = min(512, seq_len)
    queries = matmul(normed, word_query).astype(jnp.bfloat16).reshape(shape_heads)
    key_rows = matmul(normed, word_key).astype(jnp.bfloat16).reshape(shape_heads)
    value_rows = matmul(normed, word_value).astype(jnp.bfloat16).reshape(shape_heads)
    mixed_heads, log_totals = attention_forward(queries, key_rows, value_rows, doc_ids, block_rows)
    mixed_flat = mixed_heads.reshape(token_count, head_count * HD)
    attention_part = matmul(mixed_flat, word_out_proj)
    middle = input_whole + lax.psum(attention_part.astype(jnp.bfloat16), "tensor").astype(
        jnp.float32
    )
    normed_mid, pull_mid = jax.vjp(layer_norm, middle, word_norm_two)
    normed_mid = normed_mid.astype(jnp.bfloat16)
    hidden, pull_gelu = jax.vjp(gelu_tanh, matmul(normed_mid, word_up))
    hidden = hidden.astype(jnp.bfloat16)
    feedforward_part = matmul(hidden, word_down)
    full_output = middle + lax.psum(feedforward_part.astype(jnp.bfloat16), "tensor").astype(
        jnp.float32
    )
    word_output = lax.dynamic_slice_in_dim(full_output, tensor_rank * word_count, word_count, 0)
    word_output = word_output.astype(jnp.bfloat16)
    grad_down = contract_rows(hidden, cotangent)
    grad_pre = pull_gelu(contract_cols(cotangent, word_down))[0].astype(jnp.bfloat16)
    grad_up = contract_rows(normed_mid, grad_pre)
    mid_part = contract_cols(grad_pre, word_up)
    cotangent_full = cotangent.astype(jnp.float32)
    back_mid, grad_gain_two = pull_mid(
        lax.psum(mid_part.astype(jnp.bfloat16), "tensor").astype(jnp.float32)
    )
    grad_middle = cotangent_full + back_mid
    grad_middle_low = grad_middle.astype(jnp.bfloat16)
    grad_out_proj = contract_rows(mixed_flat, grad_middle_low)
    grad_mixed = (
        contract_cols(grad_middle_low, word_out_proj).astype(jnp.bfloat16).reshape(shape_heads)
    )
    grad_q, grad_k, grad_v = attention_backward(
        queries, key_rows, value_rows, doc_ids, log_totals, grad_mixed, block_rows
    )
    flat_shape = (token_count, head_count * HD)
    grad_q = grad_q.reshape(flat_shape)
    grad_k = grad_k.reshape(flat_shape)
    grad_v = grad_v.reshape(flat_shape)
    grad_query = contract_rows(normed, grad_q)
    grad_key = contract_rows(normed, grad_k)
    grad_value = contract_rows(normed, grad_v)
    first_part = (
        contract_cols(grad_q, word_query)
        + contract_cols(grad_k, word_key)
        + contract_cols(grad_v, word_value)
    )
    back_first, grad_gain_one = pull_first(
        lax.psum(first_part.astype(jnp.bfloat16), "tensor").astype(jnp.float32)
    )
    grad_input = lax.dynamic_slice_in_dim(
        grad_middle + back_first, tensor_rank * word_count, word_count, 0
    )
    gain_share = (tensor_rank == 0).astype(jnp.float32)
    grad_vectors = grad_input.astype(jnp.bfloat16)
    grad_proj = contract_rows(pooled, grad_vectors)
    grad_pooled = contract_cols(grad_vectors, char_proj)
    grad_second = (grad_pooled[:, None, :] * slot_weights[:, :, None]).reshape(
        word_count * slot_count, char_width
    )
    second_low = grad_second.astype(jnp.bfloat16)
    grad_char_down = contract_rows(char_hidden, second_low)
    grad_char_pre = pull_char_gelu(contract_cols(second_low, char_down))[0].astype(jnp.bfloat16)
    grad_char_up = contract_rows(char_normed_two, grad_char_pre)
    back_char_two, grad_char_gain_two = pull_char_two(contract_cols(grad_char_pre, char_up))
    grad_first = grad_second + back_char_two
    first_low = grad_first.astype(jnp.bfloat16)
    grad_char_out = contract_rows(char_mixed, first_low)
    grad_char_mixed = contract_cols(first_low, char_out).astype(jnp.bfloat16).reshape(shape_four)
    grad_char_probs = jnp.einsum(
        "wqhd,wkhd->whqk", grad_char_mixed, char_v, preferred_element_type=jnp.float32
    )
    char_inner = jnp.sum(char_probs * grad_char_probs, axis=-1, keepdims=True)
    grad_char_scores = (char_probs * (grad_char_probs - char_inner)).astype(jnp.bfloat16)
    flat_chars = (word_count * slot_count, char_width)
    grad_cv = jnp.einsum(
        "whqk,wqhd->wkhd", char_probs_low, grad_char_mixed, preferred_element_type=jnp.float32
    )
    grad_cv = grad_cv.astype(jnp.bfloat16).reshape(flat_chars)
    grad_cq = jnp.einsum(
        "whqk,wkhd->wqhd", grad_char_scores, char_k, preferred_element_type=jnp.float32
    )
    grad_cq = (grad_cq * char_scale).astype(jnp.bfloat16).reshape(flat_chars)
    grad_ck = jnp.einsum(
        "whqk,wqhd->wkhd", grad_char_scores, char_q, preferred_element_type=jnp.float32
    )
    grad_ck = (grad_ck * char_scale).astype(jnp.bfloat16).reshape(flat_chars)
    grad_char_query = contract_rows(char_normed, grad_cq)
    grad_char_key = contract_rows(char_normed, grad_ck)
    grad_char_value = contract_rows(char_normed, grad_cv)
    back_char_one, grad_char_gain_one = pull_char_one(
        contract_cols(grad_cq, char_query)
        + contract_cols(grad_ck, char_key)
        + contract_cols(grad_cv, char_value)
    )
    char_input_gradient = grad_first + back_char_one
    word_sums = lax.psum(
        (grad_query, grad_key, grad_value, grad_out_proj, grad_up, grad_down), "dp"
    )
    char_sums = lax.psum(
        (
            grad_char_gain_one,
            grad_char_query,
            grad_char_key,
            grad_char_value,
            grad_char_out,
            grad_char_gain_two,
            grad_char_up,
            grad_char_down,
            grad_proj,
            grad_gain_one * gain_share,
            grad_gain_two * gain_share,
        ),
        ("dp", "tensor"),
    )
    return (
        word_output,
        char_input_gradient,
        char_sums[0],
        char_sums[1],
        char_sums[2],
        char_sums[3],
        char_sums[4],
        char_sums[5],
        char_sums[6],
        char_sums[7],
        char_sums[8],
        char_sums[9],
        word_sums[0],
        word_sums[1],
        word_sums[2],
        word_sums[3],
        char_sums[10],
        word_sums[4],
        word_sums[5],
    )


def solution(mesh):
    in_specs = (
        P(("dp", "tensor"), None),
        P(("dp", "tensor")),
        P("dp", None),
        P("dp", None),
        P(),
        P(),
        P(),
        P(),
        P(),
        P(),
        P(),
        P(),
        P(),
        P(),
        P(None, "tensor"),
        P(None, "tensor"),
        P(None, "tensor"),
        P("tensor", None),
        P(),
        P(None, "tensor"),
        P("tensor", None),
    )
    out_specs = (
        P(("dp", "tensor"), None),
        P(("dp", "tensor"), None),
        P(),
        P(),
        P(),
        P(),
        P(),
        P(),
        P(),
        P(),
        P(),
        P(),
        P(None, "tensor"),
        P(None, "tensor"),
        P(None, "tensor"),
        P("tensor", None),
        P(),
        P(None, "tensor"),
        P("tensor", None),
    )
    return jax.shard_map(
        per_device, mesh=mesh, in_specs=in_specs, out_specs=out_specs, check_vma=False
    )
```

profile of v0, /device:TPU:0, one launch (start us, length us, event | category | flops | bytes accessed | tf_op | source)
XLA Modules:
  0.0 727.3 jit_solution(17585414568510393199)
XLA Ops:
  20.2 7.1 reshape.407
  27.3 3.6 convolution_convert_fusion.2
  30.9 7.1 reshape.406
  38.0 3.7 convolution_convert_fusion.3
  41.6 7.1 reshape.405
  48.7 5.8 fusion.75
  54.5 28.7 %fusion.134 = (f32[256,4,16]{2,1,0:T(4,128)S(1)}, f32[256,4,16,16]{2,3,1,0:T(8,128)S(1)}) fusion(f32[256,4,16,16]{2,3,1,0:T(8,128)S(1)} %fusion.75, pred[256,16]{1,0:T(8,128)(4,1)S(1)} %iota_compare_fusion.2), kind=kOutput, calls=%fused_computation.213 | output fusion | flops 1572879 | bytes 2166784 | tf_op jit(solution)/shard_map/sub | solution.py:175
  83.2 3.2 copy-done.21
  86.5 3.9 convert_bitcast_fusion.1
  90.4 4.2 copy.59
  94.6 7.0 reshape.408
  106.1 9.7 %multiply_convert_fusion.1 = (bf16[4096,1024]{1,0:T(8,128)(2,1)S(1)}, f32[4096,1024]{1,0:T(8,128)}) fusion(bf16[256,1024]{1,0:T(8,128)(2,1)S(1)} %copy-done, f32[4096,256]{1,0:T(8,128)S(1)} %get-tuple-element.291, f32[256]{0:T(256)S(1)} %copy-done.97, f32[4096]{0:T(1024)S(1)} %fusion.121, f32[4096]{0:T(1024)S(1)} %broadcast_multiply_fusion), kind=kOutput, calls=%fused_computation.59 | convolution fusion | flops 2189426688 | bytes 29918208 | tf_op jit(solution)/shard_map/dot_general | solution.py:24
  115.8 3.1 multiply_reduce_fusion.4
  120.1 30.8 %all-gather.2.cloned.1.call-done = bf16[1024,512]{1,0:T(8,128)(2,1)} async-done(((bf16[256,512]{1,0:T(8,128)(2,1)}), bf16[1024,512]{1,0:T(8,128)(2,1)}) %all-gather.2.cloned.1.call-update) | async-done | bytes 1048592 | tf_op jit(solution)/shard_map/all_gather | solution.py:193
  158.7 16.5 %while.47 = (s32[]{:T(128)}, bf16[2,512,2,64]{1,3,2,0:T(8,128)(2,1)S(1)}, f32[2,2,512]{2,1,0:T(2,128)}, s32[2]{0:T(128)S(1)}, s32[1024]{0:T(1024)S(1)}, /*index=...) while((s32[]{:T(128)}, ...), condition=%wide.region_12.13_spmd, body=%wide.region_9.12_spmd.sunk | while | flops 282656256 | bytes 15513803 | solution.py:73
  178.6 3.5 fusion.136
  182.1 47.9 %all-reduce.10.cloned.1.call-done = bf16[1024,512]{1,0:T(8,128)(2,1)} async-done(((bf16[1024,512]{1,0:T(8,128)(2,1)}), bf16[1024,512]{1,0:T(8,128)(2,1)}) %all-reduce.10.cloned.1.call-update) | async-done | bytes 1048592 | tf_op jit(solution)/shard_map/psum | solution.py:208
  234.0 3.1 fusion.107
  239.9 3.5 convolution_convert_fusion.6
  243.4 47.8 %all-reduce.12.cloned.1.call-done = bf16[1024,512]{1,0:T(8,128)(2,1)} async-done(((bf16[1024,512]{1,0:T(8,128)(2,1)}), bf16[1024,512]{1,0:T(8,128)(2,1)}) %all-reduce.12.cloned.1.call-update) | async-done | bytes 1048592 | tf_op jit(solution)/shard_map/psum | solution.py:227
  293.6 3.8 fusion.99
  302.9 28.6 %while.48 = (s32[]{:T(128)}, f32[1024,2,64]{0,2,1:T(8,128)S(1)}, f32[1024,2,64]{0,2,1:T(8,128)}, bf16[2,512,2,64]{1,3,2,0:T(8,128)(2,1)}, s32[2]{0:T(128)S(1)}, ...) while((s32[]{:T(128)}, f32[1024,2,64]{0,2,1:T(8,128)S(1)}, ...), condition=%wide.region_22.23_spmd.clone, body=%wide.region_20.22_spmd.clone.sunk | while | flops 689176064 | bytes 44476844 | solution.py:122
  337.5 3.4 fusion.149
  347.7 75.2 %all-reduce.18.cloned.1.call-done = (bf16[1024,512]{1,0:T(8,128)(2,1)}, bf16[1024,512]{1,0:T(8,128)(2,1)}) async-done(((bf16[1024,512]{1,0:T(8,128)(2,1)}, bf16[1024,512]{1,0:T(8,128)(2,1)}), (bf16[1024,512]{1,0:T(8,128)(2,1)}, bf16[1024,512]{1,0:T(8,128)(2,1)})) %all-reduce.18.cloned.1.call-update) | async-done | bytes 2097168 | tf_op jit(solution)/shard_map/psum | solution.py:216
  422.9 3.0 fusion.100
  431.6 15.4 %fusion.47 = bf16[4096,1024]{1,0:T(8,128)(2,1)S(1)} fusion(f32[4096,1024]{1,0:T(8,128)} %get-tuple-element.293, bf16[4096,256]{1,0:T(8,128)(2,1)S(1)} %fusion.62, bf16[1024,256]{1,0:T(8,128)(2,1)S(1)} %copy-done.54), kind=kOutput, calls=%fused_computation.58 | convolution fusion | flops 2231369728 | bytes 27787264 | tf_op jit(solution)/shard_map/dot_general | solution.py:34
  447.1 3.8 multiply_reduce_fusion.2
  458.9 3.4 reshape.414
  462.3 9.0 %convert_bitcast_fusion = bf16[256,16,4,64]{3,1,2,0:T(8,128)(2,1)} fusion(bf16[256,16,4,64]{3,2,1,0:T(4,128)(2,1)} %reshape.414, f32[256,4,16,16]{2,3,1,0:T(8,128)} %copy-done.21, f32[256,4,16]{2,1,0:T(4,128)S(1)} %copy-done.56), kind=kOutput, calls=%fused_computation.96 | convolution fusion | flops 35127296 | bytes 5308416 | tf_op jit(solution)/shard_map/whqk,wqhd->wkhd/dot_general | solution.py:278
  471.4 12.3 %multiply_reduce_fusion.1 = (f32[256,4,16]{2,1,0:T(4,128)S(1)}, f32[256,4,16,16]{2,3,1,0:T(8,128)}) fusion(f32[256,4,16,16]{2,3,1,0:T(8,128)} %copy-done.21, f32[256,4,16]{2,1,0:T(4,128)S(1)} %copy-done.56, bf16[256,16,4,64]{3,2,1,0:T(4,128)(2,1)} %reshape.405, bf16[256,16,4,64]{3,2,1,0:T(4,128)(2,1)} %reshape.414), kind=kOutput, calls=%fused_computation.63 | convolution fusion | flops 34324480 | bytes 6422528 | tf_op jit(solution)/shard_map/wqhd,wkhd->whqk/dot_general | solution.py:272
  483.7 7.6 %multiply_convert_fusion.4 = bf16[256,4,16,16]{2,3,1,0:T(8,128)(2,1)S(1)} fusion(f32[256,4,16,16]{2,3,1,0:T(8,128)} %get-tuple-element.298, f32[256,4,16]{2,1,0:T(4,128)S(1)} %get-tuple-element.297, f32[256,4,16,16]{2,3,1,0:T(8,128)} %copy-done.21, f32[256,4,16]{2,1,0:T(4,128)S(1)} %copy-done.56), kind=kLoop, calls=%fused_computation.62 | loop fusion | flops 1048576 | bytes 2752512 | tf_op jit(solution)/shard_map/convert_element_type | solution.py:276
  491.3 4.3 fusion.60
  498.0 4.2 copy.67
  502.2 7.1 reshape.415
  509.3 3.2 fusion.141
  516.0 4.1 copy.73
  520.1 7.0 reshape.417
  527.1 3.2 fusion.143
  530.2 4.2 copy.69
  534.5 7.1 reshape.416
  541.6 3.2 fusion.142
  544.8 5.7 convolution_add_fusion.1
  550.5 3.4 fusion.145
  553.9 7.5 %fusion.130 = f32[256,1024]{1,0:T(8,128)} fusion(bf16[4096,1024]{1,0:T(8,128)(2,1)} %copy-done.101, f32[4096,256]{1,0:T(8,128)S(1)} %copy-done.8, f32[256]{0:T(256)S(1)} %copy-done.98, f32[4096]{0:T(1024)S(1)} %copy-done.83, f32[4096]{0:T(1024)S(1)} %copy-done.75), kind=kOutput, calls=%fused_computation.209 | convolution fusion | flops 2151677952 | bytes 13665280 | tf_op jit(solution)/shard_map/dot_general | solution.py:28
  563.0 4.7 fusion.58
  570.4 5.9 add_add_fusion.2
  576.2 40.0 %all-reduce = (f32[256]{0:T(256)}, f32[256]{0:T(256)}, f32[512]{0:T(512)}, f32[512]{0:T(512)}) all-reduce(f32[256]{0:T(256)S(1)} %get-tuple-element.215, f32[256]{0:T(256)S(1)} %get-tuple-element.213, f32[512]{0:T(512)S(1)} %get-tuple-element.302, f32[512]{0:T(512)S(1)} %get-tuple-element.301), channel_id=1, replica_groups=mesh['dp'=8,'tensor'=4] {'dp','tensor'}, use_global_device_ids=true, to_apply=%region_32.33 | all-reduce | flops 1536 | bytes 12288 | tf_op jit(solution)/shard_map/psum | solution.py:302
  618.2 86.3 %all-reduce.14.cloned.1.call-done = (f32[256,256]{1,0:T(8,128)}, f32[256,256]{1,0:T(8,128)}, f32[256,256]{1,0:T(8,128)}, f32[256,256]{1,0:T(8,128)}, f32[256,102...) async-done(((f32[256,256]{1,0:T(8,128)}, f32[256,256]{1,0:T(8,128)}, f32[256,256]{1,0:T(8,128)}, f32[256,256]{1,0:T(8,128)}, f32[256,1024]{1,0:T(8,128)}, ...) | async-done | bytes 3670032 | tf_op jit(solution)/shard_map/psum | solution.py:302
  (361 shorter events, 136.0 us)
Async XLA Ops:
  7.2 98.9 %copy-start = (bf16[256,1024]{1,0:T(8,128)(2,1)S(1)}, bf16[256,1024]{1,0:T(8,128)(2,1)}, u32[]{:S(2)}) copy-start(bf16[256,1024]{1,0:T(8,128)(2,1)} %param.35) | copy-start | bytes 1572868
  7.2 7.1 copy-start.94
  7.2 7.3 copy-start.2
  7.2 7.3 copy-start.92
  7.2 143.7 %all-gather.2.cloned.1.call-start = ((), (), s32[]{:S(2)}) async-start(), calls=%async_computation | async-start | bytes 1310720 | tf_op jit(solution)/shard_map/all_gather | solution.py:193
  8.9 9.2 %copy-start.57 = (bf16[256,256]{1,0:T(8,128)(2,1)S(1)}, bf16[256,256]{1,0:T(8,128)(2,1)}, u32[]{:S(2)}) copy-start(bf16[256,256]{1,0:T(8,128)(2,1)} %param.31) | copy-start | bytes 393220
  14.5 101.3 %copy-start.34 = (f32[256,16]{1,0:T(8,128)}, f32[256,16]{1,0:T(8,128)S(1)}, u32[]{:S(2)}) copy-start(f32[256,16]{1,0:T(8,128)S(1)} %convert_divide_fusion) | copy-start | bytes 49156
  83.2 7.2 copy-start.55
  104.1 11.7 %copy-start.6 = (f32[4096,256]{1,0:T(8,128)}, f32[4096,256]{1,0:T(8,128)S(1)}, u32[]{:S(2)}) copy-start(f32[4096,256]{1,0:T(8,128)S(1)} %get-tuple-element.291) | copy-start | bytes 12582916
  104.1 11.7 %copy-start.74 = (f32[4096]{0:T(1024)}, f32[4096]{0:T(1024)S(1)}, u32[]{:S(2)}) copy-start(f32[4096]{0:T(1024)S(1)} %broadcast_multiply_fusion) | copy-start | bytes 49156
  106.1 9.7 %copy-start.82 = (f32[4096]{0:T(1024)}, f32[4096]{0:T(1024)S(1)}, u32[]{:S(2)}) copy-start(f32[4096]{0:T(1024)S(1)} %fusion.121) | copy-start | bytes 49156
  106.1 9.7 %copy-start.53 = (bf16[1024,256]{1,0:T(8,128)(2,1)S(1)}, bf16[1024,256]{1,0:T(8,128)(2,1)}, u32[]{:S(2)}) copy-start(bf16[1024,256]{1,0:T(8,128)(2,1)} %param.36) | copy-start | bytes 1572868
  115.8 38.3 %copy-start.90 = (f32[512]{0:T(512)S(1)}, f32[512]{0:T(512)}, u32[]{:S(2)}) copy-start(f32[512]{0:T(512)} %param.38) | copy-start | bytes 6148
  119.1 36.7 %copy-start.66 = (bf16[512,128]{1,0:T(8,128)(2,1)S(1)}, bf16[512,128]{1,0:T(8,128)(2,1)}, u32[]{:S(2)}) copy-start(bf16[512,128]{1,0:T(8,128)(2,1)} %param.41) | copy-start | bytes 393220
  119.1 37.9 %copy-start.63 = (bf16[512,128]{1,0:T(8,128)(2,1)S(1)}, bf16[512,128]{1,0:T(8,128)(2,1)}, u32[]{:S(2)}) copy-start(bf16[512,128]{1,0:T(8,128)(2,1)} %param.40) | copy-start | bytes 393220
  119.1 38.3 %copy-start.64 = (bf16[512,128]{1,0:T(8,128)(2,1)S(1)}, bf16[512,128]{1,0:T(8,128)(2,1)}, u32[]{:S(2)}) copy-start(bf16[512,128]{1,0:T(8,128)(2,1)} %param.39) | copy-start | bytes 393220
  120.0 109.9 %all-reduce.10.cloned.1.call-start = ((), (), s32[]{:S(2)}) async-start(), calls=%async_computation.1 | async-start | bytes 2097152 | tf_op jit(solution)/shard_map/psum | solution.py:208
  120.1 38.5 %copy-start.44 = (s32[1,1024]{1,0:T(1,128)S(1)}, s32[1,1024]{1,0:T(1,128)}, u32[]{:S(2)}) copy-start(s32[1,1024]{1,0:T(1,128)} %param.27) | copy-start | bytes 12292
  175.2 54.8 %copy-start.1 = (bf16[1024,512]{1,0:T(8,128)(2,1)S(1)}, bf16[1024,512]{1,0:T(8,128)(2,1)}, u32[]{:S(2)}) copy-start(bf16[1024,512]{1,0:T(8,128)(2,1)} %all-gather.2.cloned.1.call-done) | copy-start | bytes 3145732
  178.6 54.9 %copy-start.88 = (f32[512]{0:T(512)S(1)}, f32[512]{0:T(512)}, u32[]{:S(2)}) copy-start(f32[512]{0:T(512)} %param.43) | copy-start | bytes 6148
  178.6 112.5 %all-reduce.12.cloned.1.call-start = ((), (), s32[]{:S(2)}) async-start(), calls=%async_computation.2 | async-start | bytes 2097152 | tf_op jit(solution)/shard_map/psum | solution.py:227
  239.8 183.1 %all-reduce.18.cloned.1.call-start = ((), (), s32[]{:S(2)}) async-start(), calls=%async_computation.5 | async-start | bytes 4194304 | tf_op jit(solution)/shard_map/psum | solution.py:216
  337.3 280.8 %all-reduce.16.cloned.1.call-start = ((), (), s32[]{:S(2)}) async-start(), calls=%async_computation.4 | async-start | bytes 6291456 | tf_op jit(solution)/shard_map/psum | solution.py:299
  344.0 78.9 %copy-start.81 = (f32[1024]{0:T(1024)S(1)}, f32[1024]{0:T(1024)}, u32[]{:S(2)}) copy-start(f32[1024]{0:T(1024)} %copy-done.80) | copy-start | bytes 12292
  344.1 78.9 %copy-start.85 = (f32[1024]{0:T(1024)S(1)}, f32[1024]{0:T(1024)}, u32[]{:S(2)}) copy-start(f32[1024]{0:T(1024)} %copy-done.84) | copy-start | bytes 12292
  344.1 78.9 %copy-start.91 = (f32[512]{0:T(512)S(1)}, f32[512]{0:T(512)}, u32[]{:S(2)}) copy-start(f32[512]{0:T(512)} %param.38) | copy-start | bytes 6148
  346.4 79.6 %copy-start.87 = (f32[1024]{0:T(1024)S(1)}, f32[1024]{0:T(1024)}, u32[]{:S(2)}) copy-start(f32[1024]{0:T(1024)} %copy-done.86) | copy-start | bytes 12292
  347.5 82.1 %copy-start.37 = (bf16[256,512]{1,0:T(8,128)(2,1)S(1)}, bf16[256,512]{1,0:T(8,128)(2,1)}, u32[]{:S(2)}) copy-start(bf16[256,512]{1,0:T(8,128)(2,1)} %param.37) | copy-start | bytes 786436
  347.5 356.9 %all-reduce.14.cloned.1.call-start = ((), (), s32[]{:S(2)}) async-start(), calls=%async_computation.3 | async-start | bytes 7340032 | tf_op jit(solution)/shard_map/psum | solution.py:302
  431.5 15.5 %copy-start.23 = (bf16[4096,256]{1,0:T(8,128)(2,1)}, bf16[4096,256]{1,0:T(8,128)(2,1)S(1)}, u32[]{:S(2)}) copy-start(bf16[4096,256]{1,0:T(8,128)(2,1)S(1)} %fusion.62) | copy-start | bytes 6291460
  431.6 15.5 %copy-start.7 = (f32[4096,256]{1,0:T(8,128)S(1)}, f32[4096,256]{1,0:T(8,128)}, u32[]{:S(2)}) copy-start(f32[4096,256]{1,0:T(8,128)} %copy-done.6) | copy-start | bytes 12582916
  431.6 15.5 %copy-start.75 = (f32[4096]{0:T(1024)S(1)}, f32[4096]{0:T(1024)}, u32[]{:S(2)}) copy-start(f32[4096]{0:T(1024)} %copy-done.74) | copy-start | bytes 49156
  431.6 15.5 %copy-start.83 = (f32[4096]{0:T(1024)S(1)}, f32[4096]{0:T(1024)}, u32[]{:S(2)}) copy-start(f32[4096]{0:T(1024)} %copy-done.82) | copy-start | bytes 49156
  431.6 15.5 %copy-start.98 = (f32[256]{0:T(256)S(1)}, f32[256]{0:T(256)}, u32[]{:S(2)}) copy-start(f32[256]{0:T(256)} %param.34) | copy-start | bytes 3076
  483.7 7.6 %copy-start.10 = (bf16[256,16,4,64]{3,2,1,0:T(4,128)(2,1)S(1)}, bf16[256,16,4,64]{3,2,1,0:T(4,128)(2,1)}, u32[]{:S(2)}) copy-start(bf16[256,16,4,64]{3,2,1,0:T(4,128)(2,1)} %reshape.406) | copy-start | bytes 6291460
  502.2 7.1 copy-start.5
  541.6 8.9 %slice-start = ((s8[8388608]{0:T(1024)(128)(4,1)}), s8[4194304]{0:T(1024)(128)(4,1)S(1)}, s32[]{:S(2)}) async-start(s8[8388608]{0:T(1024)(128)(4,1)} %bitcast.174), calls=%async_computation.6 | async-start | bytes 8388608
  553.9 7.5 %copy-start.46 = (f32[4096]{0:T(1024)S(1)}, f32[4096]{0:T(1024)}, u32[]{:S(2)}) copy-start(f32[4096]{0:T(1024)} %copy-done.45) | copy-start | bytes 49156
  553.9 7.5 %copy-start.52 = (bf16[256,256]{1,0:T(8,128)(2,1)S(1)}, bf16[256,256]{1,0:T(8,128)(2,1)}, u32[]{:S(2)}) copy-start(bf16[256,256]{1,0:T(8,128)(2,1)} %param.32) | copy-start | bytes 393220
  553.9 7.6 %copy-start.93 = (f32[256]{0:T(256)S(1)}, f32[256]{0:T(256)}, u32[]{:S(2)}) copy-start(f32[256]{0:T(256)} %param.29) | copy-start | bytes 3076
  618.2 97.4 %copy-start.71 = (f32[512,128]{1,0:T(8,128)S(1)}, f32[512,128]{1,0:T(8,128)}, u32[]{:S(2)}) copy-start(f32[512,128]{1,0:T(8,128)} %get-tuple-element.523) | copy-start | bytes 786436
  618.2 98.1 %copy-start.70 = (f32[512,128]{1,0:T(8,128)S(1)}, f32[512,128]{1,0:T(8,128)}, u32[]{:S(2)}) copy-start(f32[512,128]{1,0:T(8,128)} %get-tuple-element.524) | copy-start | bytes 786436
  704.4 9.4 %copy-start.40 = (f32[1024,256]{1,0:T(8,128)S(1)}, f32[1024,256]{1,0:T(8,128)}, u32[]{:S(2)}) copy-start(f32[1024,256]{1,0:T(8,128)} %get-tuple-element.520) | copy-start | bytes 3145732
  704.4 10.3 %copy-start.61 = (f32[256,512]{1,0:T(8,128)S(1)}, f32[256,512]{1,0:T(8,128)}, u32[]{:S(2)}) copy-start(f32[256,512]{1,0:T(8,128)} %get-tuple-element.521) | copy-start | bytes 1572868
  704.4 12.5 %copy-start.69 = (f32[512,128]{1,0:T(8,128)S(1)}, f32[512,128]{1,0:T(8,128)}, u32[]{:S(2)}) copy-start(f32[512,128]{1,0:T(8,128)} %get-tuple-element.525) | copy-start | bytes 786436
  706.2 11.4 %copy-start.68 = (f32[128,512]{1,0:T(8,128)S(1)}, f32[128,512]{1,0:T(8,128)}, u32[]{:S(2)}) copy-start(f32[128,512]{1,0:T(8,128)} %get-tuple-element.526) | copy-start | bytes 786436
  707.9 10.4 %copy-start.39 = (f32[512,512]{1,0:T(8,128)S(1)}, f32[512,512]{1,0:T(8,128)}, u32[]{:S(2)}) copy-start(f32[512,512]{1,0:T(8,128)} %get-tuple-element.528) | copy-start | bytes 3145732
  711.4 8.0 %copy-start.38 = (f32[512,512]{1,0:T(8,128)S(1)}, f32[512,512]{1,0:T(8,128)}, u32[]{:S(2)}) copy-start(f32[512,512]{1,0:T(8,128)} %get-tuple-element.529) | copy-start | bytes 3145732
  (68 other events, 241.9 us)
Sparse Core Ops, SparseCore 0:
  120.2 30.6 all-gather.1
  178.7 51.2 all-reduce.9
  239.9 51.1 all-reduce.11
  337.5 85.4 all-reduce.17
  427.9 69.0 all-reduce.15
  561.6 142.8 all-reduce.13
where the time goes:
time: 738 us; the launch traced here: 727 us
  waiting for transfers between devices  288 us (39%)
  matrix products  176 us (24%)
  local copies, waits for them, and re-layouts  106 us (14%)
  other arithmetic  94.6 us (13%)
  blocking collectives  40 us (5%)
  between operations  15.6 us (2%)
    psum x1, waiting for transfers between devices, per_device(): lax.psum((grad_char_gain_one, grad_char_query, grad_char_key, grad_char_v...  86.3 us
    psum x1, waiting for transfers between devices, per_device(): lax.psum(feedforward_part.astype(jnp.bfloat16), 'tensor')  75.2 us
    psum x1, waiting for transfers between devices, per_device(): lax.psum(attention_part.astype(jnp.bfloat16), 'tensor').astype(jnp.float32)  47.9 us
    psum x1, waiting for transfers between devices, per_device(): lax.psum(mid_part.astype(jnp.bfloat16), 'tensor').astype(jnp.float32)  47.8 us
    dot_general x13, matrix products, contract_cols(): lax.dot_general(left, right, (((1,), (1,)), ((), ())), preferred_element_...  43 us
    psum x1, blocking collectives, per_device(): lax.psum((grad_char_gain_one, grad_char_query, grad_char_key, grad_char_v...  40 us
    dot_general x13, matrix products, matmul(): return jnp.dot(left, right, preferred_element_type=jnp.float32)  37.2 us
    dot_general x13, matrix products, contract_rows(): lax.dot_general(left, right, (((0,), (0,)), ((), ())), preferred_element_...  32.8 us
  transfers between devices with their start and end apart: 6, of which 5 were waited for; matrix products, arithmetic and copies ran while one was open for 23% of the time, Pallas kernels for 0%

commit v1 on v0

--- a/solution.py
+++ b/solution.py
@@ -8,6 +8,12 @@
 CHD = 64
 EPSILON = 1e-05
 NEG_LARGE = -1e30
+
+
+def spread_chains(matrix, where_dim):
+    u1 = list(matrix.shape[1:])
+    u1[where_dim] *= matrix.shape[0]
+    return jnp.moveaxis(matrix, 0, where_dim).reshape(u1)
 
 
 def layer_norm(values, gain_vector):
@@ -190,7 +196,31 @@
     )
     pooled = pooled.astype(jnp.bfloat16)
     word_vectors = matmul(pooled, char_proj).astype(jnp.bfloat16)
-    input_whole = lax.all_gather(word_vectors, "tensor", axis=0, tiled=True).astype(jnp.float32)
+
+    def match_samples_all_up(shard_axis, k_dim, mine_x):
+        n_dev_all = lax.axis_size(shard_axis)
+        entries = [(b, (b + 1) % n_dev_all) for b in range(n_dev_all)]
+        samples = [(h, i) for i, h in entries]
+        b_next, front = ([], [])
+        k0 = 0
+        while k0 < n_dev_all - 1:
+            if k0 % 2 == 0:
+                b_next.append(
+                    lax.ppermute(
+                        b_next[-1] if b_next else mine_x, perm=entries, axis_name=shard_axis
+                    )
+                )
+            else:
+                front.append(
+                    lax.ppermute(front[-1] if front else mine_x, perm=samples, axis_name=shard_axis)
+                )
+            k0 += 1
+        k_now = jnp.stack([*b_next[::-1], mine_x, *front], axis=0)
+        piece_next = lax.axis_index(shard_axis) - len(b_next)
+        k_now = k_now[(jnp.arange(n_dev_all) - piece_next) % n_dev_all]
+        return spread_chains(k_now, k_dim)
+
+    input_whole = match_samples_all_up("tensor", 0, word_vectors).astype(jnp.float32)
     normed_whole, pull_first = jax.vjp(layer_norm, input_whole, word_norm_one)
     normed = normed_whole.astype(jnp.bfloat16)
     sequences = doc_ids.shape[0]

time: 738 us -> 716 us (0.970)
  waiting for transfers between devices: 288 us -> 274 us
  matrix products: 176 us -> 168 us
    all_gather x1 -> x0, waiting for transfers between devices: 30.8 us -> none  [per_device(): lax.all_gather(word_vectors, 'tensor', axis=0, tiled=True)]
    ppermute x0 -> x3, waiting for transfers between devices: none -> 17.5 us  [the longest x2 13.2 us: match_samples_all_up(): lax.ppermute(b_next[-1] if b_next else mine_x, perm=entries, axis_name=sh...]
    unnamed x215 -> x223, local copies, waits for them, and re-layouts: 29.2 us -> 27.6 us
  transfers between devices with their start and end apart: 6 -> 8, of which waited for: 5 -> 7; matrix products, arithmetic and copies ran while one was open for 23% -> 24% of each run, Pallas kernels for 0% -> 0%
where the time goes in v1:
time: 716 us; the launch traced here: 705 us
  waiting for transfers between devices  274 us (38%)
  matrix products  168 us (23%)
  local copies, waits for them, and re-layouts  103 us (14%)
  other arithmetic  92 us (13%)
  blocking collectives  40 us (6%)
  between operations  15.4 us (2%)
    psum x1, waiting for transfers between devices, per_device(): lax.psum((grad_char_gain_one, grad_char_query, grad_char_key, grad_char_v...  86.3 us
    psum x1, waiting for transfers between devices, per_device(): lax.psum(feedforward_part.astype(jnp.bfloat16), 'tensor')  74.6 us
    psum x1, waiting for transfers between devices, per_device(): lax.psum(attention_part.astype(jnp.bfloat16), 'tensor').astype(jnp.float32)  48.2 us
    psum x1, waiting for transfers between devices, per_device(): lax.psum(mid_part.astype(jnp.bfloat16), 'tensor').astype(jnp.float32)  47.8 us
    dot_general x13, matrix products, contract_cols(): lax.dot_general(left, right, (((1,), (1,)), ((), ())), preferred_element_...  41 us
    psum x1, blocking collectives, per_device(): lax.psum((grad_char_gain_one, grad_char_query, grad_char_key, grad_char_v...  40 us
    dot_general x13, matrix products, matmul(): return jnp.dot(left, right, preferred_element_type=jnp.float32)  36.6 us
    dot_general x13, matrix products, contract_rows(): lax.dot_general(left, right, (((0,), (0,)), ((), ())), preferred_element_...  34.2 us
  transfers between devices with their start and end apart: 8, of which 7 were waited for; matrix products, arithmetic and copies ran while one was open for 24% of the time, Pallas kernels for 0%

profile of v1, /device:TPU:0, one launch (start us, length us, event | category | flops | bytes accessed | tf_op | source)
XLA Modules:
  0.0 705.2 jit_solution(2421125756293345555)
XLA Ops:
  13.9 3.2 fusion.55
  17.2 3.6 convolution_convert_fusion.1
  20.8 7.1 %reshape.667 = bf16[256,16,4,64]{3,2,1,0:T(4,128)(2,1)} reshape(bf16[4096,256]{1,0:T(8,128)(2,1)} %convolution_convert_fusion.1) | data formatting | bytes 4194304 | tf_op jit(solution)/shard_map/reshape | solution.py:173
  27.9 3.6 convolution_convert_fusion.2
  31.5 7.1 %reshape.666 = bf16[256,16,4,64]{3,2,1,0:T(4,128)(2,1)} reshape(bf16[4096,256]{1,0:T(8,128)(2,1)} %convolution_convert_fusion.2) | data formatting | bytes 4194304 | tf_op jit(solution)/shard_map/reshape | solution.py:172
  38.6 3.6 convolution_convert_fusion.3
  42.2 7.1 %reshape.665 = bf16[256,16,4,64]{3,2,1,0:T(4,128)(2,1)} reshape(bf16[4096,256]{1,0:T(8,128)(2,1)} %convolution_convert_fusion.3) | data formatting | bytes 4194304 | tf_op jit(solution)/shard_map/reshape | solution.py:174
  49.3 5.8 fusion.75
  55.1 28.7 %fusion.141 = (f32[256,4,16]{2,1,0:T(4,128)S(1)}, f32[256,4,16,16]{2,3,1,0:T(8,128)S(1)}) fusion(f32[256,4,16,16]{2,3,1,0:T(8,128)S(1)} %fusion.75, pred[256,16]{1,0:T(8,128)(4,1)S(1)} %iota_compare_fusion.2), kind=kOutput, calls=%fused_computation.228 | output fusion | flops 1572879 | bytes 2166784 | tf_op jit(solution)/shard_map/sub | solution.py:181
  83.8 3.3 copy-done.21
  87.1 3.9 convert_bitcast_fusion.1
  91.0 4.3 copy.59
  95.2 7.0 reshape.668
  106.7 9.7 %multiply_convert_fusion.1 = (bf16[4096,1024]{1,0:T(8,128)(2,1)S(1)}, f32[4096,1024]{1,0:T(8,128)}) fusion(bf16[256,1024]{1,0:T(8,128)(2,1)S(1)} %copy-done, f32[4096,256]{1,0:T(8,128)S(1)} %get-tuple-element.295, f32[256]{0:T(256)S(1)} %copy-done.99, f32[4096]{0:T(1024)S(1)} %fusion.124, f32[4096]{0:T(1024)S(1)} %broadcast_multiply_fusion), kind=kOutput, calls=%fused_computation.60 | convolution fusion | flops 2189426688 | bytes 29918208 | tf_op jit(solution)/shard_map/dot_general | solution.py:30
  116.4 3.1 multiply_reduce_fusion.4
  125.1 7.1 %collective-permute-done = bf16[256,512]{1,0:T(8,128)(2,1)S(1)} collective-permute-done((bf16[256,512]{1,0:T(8,128)(2,1)S(1)}, bf16[256,512]{1,0:T(8,128)(2,1)S(1)}, u32[]{:S(2)}, u32[]{:S(2)}) %collective-permute-start) | collective-permute-done | bytes 262176 | tf_op jit(solution)/shard_map/ppermute | solution.py:209
  132.2 4.3 collective-permute-done.2
  136.5 6.1 collective-permute-done.1
  147.7 12.8 %while.47 = (s32[]{:T(128)}, bf16[2,512,2,64]{1,3,2,0:T(8,128)(2,1)}, f32[2,2,512]{2,1,0:T(2,128)S(1)}, s32[2]{0:T(128)S(1)}, s32[1024]{0:T(1024)S(1)}, /*index=...) while((s32[]{:T(128)}, ...), condition=%wide.region_12.13_spmd, body=%wide.region_9.12_spmd.sunk | while | flops 282656256 | bytes 15513803 | solution.py:79
  168.2 48.2 %all-reduce.10.cloned.1.call-done = bf16[1024,512]{1,0:T(8,128)(2,1)} async-done(((bf16[1024,512]{1,0:T(8,128)(2,1)}), bf16[1024,512]{1,0:T(8,128)(2,1)}) %all-reduce.10.cloned.1.call-update) | async-done | bytes 1048592 | tf_op jit(solution)/shard_map/psum | solution.py:238
  227.0 3.5 convolution_convert_fusion.6
  230.5 47.8 %all-reduce.12.cloned.1.call-done = bf16[1024,512]{1,0:T(8,128)(2,1)} async-done(((bf16[1024,512]{1,0:T(8,128)(2,1)}), bf16[1024,512]{1,0:T(8,128)(2,1)}) %all-reduce.12.cloned.1.call-update) | async-done | bytes 1048592 | tf_op jit(solution)/shard_map/psum | solution.py:257
  280.4 3.6 fusion.95
  288.0 24.3 %while.48 = (s32[]{:T(128)}, f32[1024,2,64]{0,2,1:T(8,128)S(1)}, f32[1024,2,64]{0,2,1:T(8,128)}, bf16[2,512,2,64]{1,3,2,0:T(8,128)(2,1)S(1)}, s32[2]{0:T(128)S(1...) while((s32[]{:T(128)}, f32[1024,2,64]{0,2,1:T(8,128)S(1)}, ...), condition=%wide.region_22.23_spmd.clone, body=%wide.region_20.22_spmd.clone.sunk | while | flops 689176064 | bytes 43428240 | solution.py:128
  317.0 3.6 fusion.156
  327.4 74.6 %all-reduce.18.cloned.1.call-done = (bf16[1024,512]{1,0:T(8,128)(2,1)}, bf16[1024,512]{1,0:T(8,128)(2,1)}) async-done(((bf16[1024,512]{1,0:T(8,128)(2,1)}, bf16[1024,512]{1,0:T(8,128)(2,1)}), (bf16[1024,512]{1,0:T(8,128)(2,1)}, bf16[1024,512]{1,0:T(8,128)(2,1)})) %all-reduce.18.cloned.1.call-update) | async-done | bytes 2097168 | tf_op jit(solution)/shard_map/psum | solution.py:246
  410.7 15.4 %fusion.47 = bf16[4096,1024]{1,0:T(8,128)(2,1)S(1)} fusion(f32[4096,1024]{1,0:T(8,128)} %get-tuple-element.297, bf16[4096,256]{1,0:T(8,128)(2,1)S(1)} %fusion.62, bf16[1024,256]{1,0:T(8,128)(2,1)S(1)} %copy-done.52), kind=kOutput, calls=%fused_computation.59 | convolution fusion | flops 2231369728 | bytes 27787264 | tf_op jit(solution)/shard_map/dot_general | solution.py:40
  426.2 3.8 multiply_reduce_fusion.2
  437.9 3.5 reshape.674
  441.4 9.0 %convert_bitcast_fusion = bf16[256,16,4,64]{3,1,2,0:T(8,128)(2,1)} fusion(bf16[256,16,4,64]{3,2,1,0:T(4,128)(2,1)} %reshape.674, f32[256,4,16,16]{2,3,1,0:T(8,128)} %copy-done.21, f32[256,4,16]{2,1,0:T(4,128)S(1)} %copy-done.54), kind=kOutput, calls=%fused_computation.97 | convolution fusion | flops 35127296 | bytes 5308416 | tf_op jit(solution)/shard_map/whqk,wqhd->wkhd/dot_general | solution.py:308
  450.4 12.3 %multiply_reduce_fusion.1 = (f32[256,4,16]{2,1,0:T(4,128)S(1)}, f32[256,4,16,16]{2,3,1,0:T(8,128)}) fusion(f32[256,4,16,16]{2,3,1,0:T(8,128)} %copy-done.21, f32[256,4,16]{2,1,0:T(4,128)S(1)} %copy-done.54, bf16[256,16,4,64]{3,2,1,0:T(4,128)(2,1)} %reshape.665, bf16[256,16,4,64]{3,2,1,0:T(4,128)(2,1)} %reshape.674), kind=kOutput, calls=%fused_computation.64 | convolution fusion | flops 34324480 | bytes 6422528 | tf_op jit(solution)/shard_map/wqhd,wkhd->whqk/dot_general | solution.py:302
  462.7 7.6 %multiply_convert_fusion.4 = bf16[256,4,16,16]{2,3,1,0:T(8,128)(2,1)S(1)} fusion(f32[256,4,16,16]{2,3,1,0:T(8,128)} %get-tuple-element.302, f32[256,4,16]{2,1,0:T(4,128)S(1)} %get-tuple-element.301, f32[256,4,16,16]{2,3,1,0:T(8,128)} %copy-done.21, f32[256,4,16]{2,1,0:T(4,128)S(1)} %copy-done.54), kind=kLoop, calls=%fused_computation.63 | loop fusion | flops 1048576 | bytes 2752512 | tf_op jit(solution)/shard_map/convert_element_type | solution.py:306
  470.4 4.3 fusion.60
  477.1 4.2 copy.67
  481.3 6.0 reshape.675
  493.8 4.2 copy.73
  497.9 6.0 reshape.677
  503.9 3.8 fusion.150
  507.7 4.2 copy.69
  512.0 7.1 %reshape.676 = bf16[4096,256]{1,0:T(8,128)(2,1)} reshape(bf16[256,16,4,64]{3,2,1,0:T(4,128)(2,1)} %copy.69) | data formatting | bytes 4194304 | tf_op jit(solution)/shard_map/reshape | solution.py:319
  519.1 3.8 fusion.149
  522.9 5.7 convolution_add_fusion.1
  528.7 3.4 fusion.152
  532.1 7.5 %fusion.137 = f32[256,1024]{1,0:T(8,128)} fusion(bf16[4096,1024]{1,0:T(8,128)(2,1)} %copy-done.103, f32[4096,256]{1,0:T(8,128)S(1)} %copy-done.5, f32[256]{0:T(256)S(1)} %copy-done.100, f32[4096]{0:T(1024)S(1)} %copy-done.80, f32[4096]{0:T(1024)S(1)} %copy-done.74), kind=kOutput, calls=%fused_computation.224 | convolution fusion | flops 2151677952 | bytes 13665280 | tf_op jit(solution)/shard_map/dot_general | solution.py:34
  541.2 4.7 fusion.58
  548.5 5.9 add_add_fusion.2
  554.4 40.0 %all-reduce = (f32[256]{0:T(256)}, f32[256]{0:T(256)}, f32[512]{0:T(512)}, f32[512]{0:T(512)}) all-reduce(f32[256]{0:T(256)S(1)} %get-tuple-element.215, f32[256]{0:T(256)S(1)} %get-tuple-element.213, f32[512]{0:T(512)S(1)} %get-tuple-element.306, f32[512]{0:T(512)S(1)} %get-tuple-element.305), channel_id=1, replica_groups=mesh['dp'=8,'tensor'=4] {'dp','tensor'}, use_global_device_ids=true, to_apply=%region_32.33 | all-reduce | flops 1536 | bytes 12288 | tf_op jit(solution)/shard_map/psum | solution.py:332
  596.3 86.3 %all-reduce.14.cloned.1.call-done = (f32[256,256]{1,0:T(8,128)}, f32[256,256]{1,0:T(8,128)}, f32[256,256]{1,0:T(8,128)}, f32[256,256]{1,0:T(8,128)}, f32[256,102...) async-done(((f32[256,256]{1,0:T(8,128)}, f32[256,256]{1,0:T(8,128)}, f32[256,256]{1,0:T(8,128)}, f32[256,256]{1,0:T(8,128)}, f32[256,1024]{1,0:T(8,128)}, ...) | async-done | bytes 3670032 | tf_op jit(solution)/shard_map/psum | solution.py:332
  (374 shorter events, 134.5 us)
Async XLA Ops:
  7.2 99.4 %copy-start = (bf16[256,1024]{1,0:T(8,128)(2,1)S(1)}, bf16[256,1024]{1,0:T(8,128)(2,1)}, u32[]{:S(2)}) copy-start(bf16[256,1024]{1,0:T(8,128)(2,1)} %param.35) | copy-start | bytes 1572868
  7.2 6.7 copy-start.1
  7.2 209.2 %all-reduce.10.cloned.1.call-start = ((), (), s32[]{:S(2)}) async-start(), calls=%async_computation | async-start | bytes 2097152 | tf_op jit(solution)/shard_map/psum | solution.py:238
  8.9 8.2 %copy-start.55 = (bf16[256,256]{1,0:T(8,128)(2,1)S(1)}, bf16[256,256]{1,0:T(8,128)(2,1)}, u32[]{:S(2)}) copy-start(bf16[256,256]{1,0:T(8,128)(2,1)} %param.31) | copy-start | bytes 393220
  13.9 102.4 %copy-start.34 = (f32[256,16]{1,0:T(8,128)}, f32[256,16]{1,0:T(8,128)S(1)}, u32[]{:S(2)}) copy-start(f32[256,16]{1,0:T(8,128)S(1)} %convert_divide_fusion) | copy-start | bytes 49156
  20.8 7.1 %copy-start.47 = (bf16[256,256]{1,0:T(8,128)(2,1)S(1)}, bf16[256,256]{1,0:T(8,128)(2,1)}, u32[]{:S(2)}) copy-start(bf16[256,256]{1,0:T(8,128)(2,1)} %param.30) | copy-start | bytes 393220
  31.5 7.1 %copy-start.49 = (bf16[256,256]{1,0:T(8,128)(2,1)S(1)}, bf16[256,256]{1,0:T(8,128)(2,1)}, u32[]{:S(2)}) copy-start(bf16[256,256]{1,0:T(8,128)(2,1)} %param.32) | copy-start | bytes 393220
  83.8 7.2 %copy-start.53 = (f32[256,4,16]{2,1,0:T(4,128)}, f32[256,4,16]{2,1,0:T(4,128)S(1)}, u32[]{:S(2)}) copy-start(f32[256,4,16]{2,1,0:T(4,128)S(1)} %get-tuple-element.292) | copy-start | bytes 196612
  95.2 7.0 copy-start.45
  104.6 11.7 %copy-start.3 = (f32[4096,256]{1,0:T(8,128)}, f32[4096,256]{1,0:T(8,128)S(1)}, u32[]{:S(2)}) copy-start(f32[4096,256]{1,0:T(8,128)S(1)} %get-tuple-element.295) | copy-start | bytes 12582916
  104.7 11.7 %copy-start.73 = (f32[4096]{0:T(1024)}, f32[4096]{0:T(1024)S(1)}, u32[]{:S(2)}) copy-start(f32[4096]{0:T(1024)S(1)} %broadcast_multiply_fusion) | copy-start | bytes 49156
  106.6 9.7 %copy-start.79 = (f32[4096]{0:T(1024)}, f32[4096]{0:T(1024)S(1)}, u32[]{:S(2)}) copy-start(f32[4096]{0:T(1024)S(1)} %fusion.124) | copy-start | bytes 49156
  106.7 9.7 %copy-start.51 = (bf16[1024,256]{1,0:T(8,128)(2,1)S(1)}, bf16[1024,256]{1,0:T(8,128)(2,1)}, u32[]{:S(2)}) copy-start(bf16[1024,256]{1,0:T(8,128)(2,1)} %param.36) | copy-start | bytes 1572868
  119.6 25.2 %copy-start.90 = (f32[512]{0:T(512)S(1)}, f32[512]{0:T(512)}, u32[]{:S(2)}) copy-start(f32[512]{0:T(512)} %param.38) | copy-start | bytes 6148
  119.9 12.3 %collective-permute-start = (bf16[256,512]{1,0:T(8,128)(2,1)S(1)}, bf16[256,512]{1,0:T(8,128)(2,1)S(1)}, u32[]{:S(2)}, u32[]{:S(2)}) collective-permute-start(bf16[256,512]{1,0:T(8,128)(2,1)S(1)} %convolution_convert_fusion.11), channel_id=1, source_target_pairs={{0,1},{1,2},{2,3},{3,0},{4,5},{5,6},{6,7},{7,4},{8,9},{9,10},{10,1... | collective-permute-start | bytes 786440 | tf_op jit(solution)/shard_map/ppermute | solution.py:209
  123.0 13.5 %collective-permute-start.2 = (bf16[256,512]{1,0:T(8,128)(2,1)S(1)}, bf16[256,512]{1,0:T(8,128)(2,1)S(1)}, u32[]{:S(2)}, u32[]{:S(2)}) collective-permute-start(bf16[256,512]{1,0:T(8,128)(2,1)S(1)} %convolution_convert_fusion.11), channel_id=1, source_target_pairs={{1,0},{2,1},{3,2},{0,3},{5,4},{6,5},{7,6},{4,7},{9,8},{10,9},{11,1... | collective-permute-start | bytes 786440 | tf_op jit(solution)/shard_map/ppermute | solution.py:215
  132.2 10.4 %collective-permute-start.1 = (bf16[256,512]{1,0:T(8,128)(2,1)S(1)}, bf16[256,512]{1,0:T(8,128)(2,1)S(1)}, u32[]{:S(2)}, u32[]{:S(2)}) collective-permute-start(bf16[256,512]{1,0:T(8,128)(2,1)S(1)} %collective-permute-done), channel_id=1, source_target_pairs={{0,1},{1,2},{2,3},{3,0},{4,5},{5,6},{6,7},{7,4},{8,9},{9,10},{10,1... | collective-permute-start | bytes 786440 | tf_op jit(solution)/shard_map/ppermute | solution.py:209
  160.5 56.0 %copy-start.85 = (f32[2,2,512]{2,1,0:T(2,128)}, f32[2,2,512]{2,1,0:T(2,128)S(1)}, u32[]{:S(2)}) copy-start(f32[2,2,512]{2,1,0:T(2,128)S(1)} %get-tuple-element.475) | copy-start | bytes 24580
  160.5 57.7 %copy-start.15 = (bf16[1024,2,64]{0,2,1:T(8,128)(2,1)}, bf16[1024,2,64]{0,2,1:T(8,128)(2,1)S(1)}, u32[]{:S(2)}) copy-start(bf16[1024,2,64]{0,2,1:T(8,128)(2,1)S(1)} %get-tuple-element.568) | copy-start | bytes 786436
  160.5 57.7 %copy-start.17 = (bf16[1024,2,64]{0,2,1:T(8,128)(2,1)}, bf16[1024,2,64]{0,2,1:T(8,128)(2,1)S(1)}, u32[]{:S(2)}) copy-start(bf16[1024,2,64]{0,2,1:T(8,128)(2,1)S(1)} %get-tuple-element.569) | copy-start | bytes 786436
  165.1 113.2 %all-reduce.12.cloned.1.call-start = ((), (), s32[]{:S(2)}) async-start(), calls=%async_computation.1 | async-start | bytes 2097152 | tf_op jit(solution)/shard_map/psum | solution.py:257
  226.9 175.0 %all-reduce.18.cloned.1.call-start = ((), (), s32[]{:S(2)}) async-start(), calls=%async_computation.4 | async-start | bytes 4194304 | tf_op jit(solution)/shard_map/psum | solution.py:246
  288.0 25.9 %copy-start.62 = (bf16[512,128]{1,0:T(8,128)(2,1)S(1)}, bf16[512,128]{1,0:T(8,128)(2,1)}, u32[]{:S(2)}) copy-start(bf16[512,128]{1,0:T(8,128)(2,1)} %param.40) | copy-start | bytes 393220
  316.4 279.9 %all-reduce.16.cloned.1.call-start = ((), (), s32[]{:S(2)}) async-start(), calls=%async_computation.3 | async-start | bytes 6291456 | tf_op jit(solution)/shard_map/psum | solution.py:329
  323.7 78.3 %copy-start.82 = (f32[1,2,4,128]{3,1,2,0:T(2,128)S(1)}, f32[1,2,4,128]{3,1,2,0:T(2,128)}, u32[]{:S(2)}) copy-start(f32[1,2,4,128]{3,1,2,0:T(2,128)} %copy-done.81) | copy-start | bytes 12292
  323.7 78.3 %copy-start.84 = (f32[1024]{0:T(1024)S(1)}, f32[1024]{0:T(1024)}, u32[]{:S(2)}) copy-start(f32[1024]{0:T(1024)} %copy-done.83) | copy-start | bytes 12292
  326.1 78.9 %copy-start.89 = (f32[1,2,4,128]{3,1,2,0:T(2,128)S(1)}, f32[1,2,4,128]{3,1,2,0:T(2,128)}, u32[]{:S(2)}) copy-start(f32[1,2,4,128]{3,1,2,0:T(2,128)} %copy-done.88) | copy-start | bytes 12292
  327.1 81.4 %copy-start.37 = (bf16[256,512]{1,0:T(8,128)(2,1)S(1)}, bf16[256,512]{1,0:T(8,128)(2,1)}, u32[]{:S(2)}) copy-start(bf16[256,512]{1,0:T(8,128)(2,1)} %param.37) | copy-start | bytes 786436
  327.1 355.4 %all-reduce.14.cloned.1.call-start = ((), (), s32[]{:S(2)}) async-start(), calls=%async_computation.2 | async-start | bytes 7340032 | tf_op jit(solution)/shard_map/psum | solution.py:332
  410.6 15.5 %copy-start.23 = (bf16[4096,256]{1,0:T(8,128)(2,1)}, bf16[4096,256]{1,0:T(8,128)(2,1)S(1)}, u32[]{:S(2)}) copy-start(bf16[4096,256]{1,0:T(8,128)(2,1)S(1)} %fusion.62) | copy-start | bytes 6291460
  410.6 15.5 %copy-start.4 = (f32[4096,256]{1,0:T(8,128)S(1)}, f32[4096,256]{1,0:T(8,128)}, u32[]{:S(2)}) copy-start(f32[4096,256]{1,0:T(8,128)} %copy-done.3) | copy-start | bytes 12582916
  410.6 15.5 %copy-start.74 = (f32[4096]{0:T(1024)S(1)}, f32[4096]{0:T(1024)}, u32[]{:S(2)}) copy-start(f32[4096]{0:T(1024)} %copy-done.73) | copy-start | bytes 49156
  410.6 15.5 %copy-start.80 = (f32[4096]{0:T(1024)S(1)}, f32[4096]{0:T(1024)}, u32[]{:S(2)}) copy-start(f32[4096]{0:T(1024)} %copy-done.79) | copy-start | bytes 49156
  410.7 15.5 %copy-start.100 = (f32[256]{0:T(256)S(1)}, f32[256]{0:T(256)}, u32[]{:S(2)}) copy-start(f32[256]{0:T(256)} %param.34) | copy-start | bytes 3076
  462.7 7.6 %copy-start.7 = (bf16[256,16,4,64]{3,2,1,0:T(4,128)(2,1)S(1)}, bf16[256,16,4,64]{3,2,1,0:T(4,128)(2,1)}, u32[]{:S(2)}) copy-start(bf16[256,16,4,64]{3,2,1,0:T(4,128)(2,1)} %reshape.666) | copy-start | bytes 6291460
  503.9 8.1 %copy-start.20 = (bf16[4096,256]{1,0:T(8,128)(2,1)}, bf16[4096,256]{1,0:T(8,128)(2,1)S(1)}, u32[]{:S(2)}) copy-start(bf16[4096,256]{1,0:T(8,128)(2,1)S(1)} %reshape.677) | copy-start | bytes 6291460
  519.1 9.6 %slice-start = ((s8[8388608]{0:T(1024)(128)(4,1)}), s8[4194304]{0:T(1024)(128)(4,1)S(1)}, s32[]{:S(2)}) async-start(s8[8388608]{0:T(1024)(128)(4,1)} %bitcast.219), calls=%async_computation.5 | async-start | bytes 8388608
  532.1 7.5 %copy-start.44 = (f32[4096]{0:T(1024)S(1)}, f32[4096]{0:T(1024)}, u32[]{:S(2)}) copy-start(f32[4096]{0:T(1024)} %copy-done.43) | copy-start | bytes 49156
  532.1 7.5 %copy-start.50 = (bf16[256,256]{1,0:T(8,128)(2,1)S(1)}, bf16[256,256]{1,0:T(8,128)(2,1)}, u32[]{:S(2)}) copy-start(bf16[256,256]{1,0:T(8,128)(2,1)} %param.32) | copy-start | bytes 393220
  532.1 7.5 %copy-start.95 = (f32[256]{0:T(256)S(1)}, f32[256]{0:T(256)}, u32[]{:S(2)}) copy-start(f32[256]{0:T(256)} %param.29) | copy-start | bytes 3076
  596.3 97.4 %copy-start.70 = (f32[512,128]{1,0:T(8,128)S(1)}, f32[512,128]{1,0:T(8,128)}, u32[]{:S(2)}) copy-start(f32[512,128]{1,0:T(8,128)} %get-tuple-element.527) | copy-start | bytes 786436
  596.3 98.1 %copy-start.69 = (f32[512,128]{1,0:T(8,128)S(1)}, f32[512,128]{1,0:T(8,128)}, u32[]{:S(2)}) copy-start(f32[512,128]{1,0:T(8,128)} %get-tuple-element.528) | copy-start | bytes 786436
  682.6 9.4 %copy-start.40 = (f32[1024,256]{1,0:T(8,128)S(1)}, f32[1024,256]{1,0:T(8,128)}, u32[]{:S(2)}) copy-start(f32[1024,256]{1,0:T(8,128)} %get-tuple-element.524) | copy-start | bytes 3145732
  682.6 10.3 %copy-start.59 = (f32[256,512]{1,0:T(8,128)S(1)}, f32[256,512]{1,0:T(8,128)}, u32[]{:S(2)}) copy-start(f32[256,512]{1,0:T(8,128)} %get-tuple-element.525) | copy-start | bytes 1572868
  682.6 12.5 %copy-start.68 = (f32[512,128]{1,0:T(8,128)S(1)}, f32[512,128]{1,0:T(8,128)}, u32[]{:S(2)}) copy-start(f32[512,128]{1,0:T(8,128)} %get-tuple-element.529) | copy-start | bytes 786436
  684.4 11.4 %copy-start.67 = (f32[128,512]{1,0:T(8,128)S(1)}, f32[128,512]{1,0:T(8,128)}, u32[]{:S(2)}) copy-start(f32[128,512]{1,0:T(8,128)} %get-tuple-element.530) | copy-start | bytes 786436
  686.1 10.4 %copy-start.39 = (f32[512,512]{1,0:T(8,128)S(1)}, f32[512,512]{1,0:T(8,128)}, u32[]{:S(2)}) copy-start(f32[512,512]{1,0:T(8,128)} %get-tuple-element.532) | copy-start | bytes 3145732
  689.5 8.0 %copy-start.38 = (f32[512,512]{1,0:T(8,128)S(1)}, f32[512,512]{1,0:T(8,128)}, u32[]{:S(2)}) copy-start(f32[512,512]{1,0:T(8,128)} %get-tuple-element.533) | copy-start | bytes 3145732
  (71 other events, 230.1 us)
Sparse Core Ops, SparseCore 0:
  165.2 51.2 all-reduce.9
  227.1 51.1 all-reduce.11
  316.5 85.4 all-reduce.17
  407.0 69.0 all-reduce.15
  539.7 142.8 all-reduce.13
